TPU v7x, 32 devices: a whole 2x2x4 slice. The times are simulated.
32 devices in a mesh: pair: 8 (over z, y), row: 4 (over x, core).
Axes of the slice: x: 2, y: 2, z: 4, core: 2. Of those that a mesh axis runs over, the one named last changes fastest.
Arguments:
- snapshots: float32 [1024, 16384], P('pair', 'row'), may hold values from -50 to 50
- live_rows: int32 [4], P('row'), may hold values from 2048 to 4096, as said below
Outputs:
- rotated: float32 [1024, 16384], P('pair', 'row')
Inputs may be any that keep to these rules, and one draw needn't show every extreme that they name: Row slot s of row index r is live when s < live_rows[r]; every draw has a row index with all 4096 slots live.
All inputs are finite; a program needn't handle non-finite values.
Results may differ from a plain program's by a relative error of at most 0.0003.
Values sent between devices are 32-bit elements; how exact they have to be, the bound alone decides.
A program may use at most 64 MiB of HBM per device.

v0:
```python
import jax
import jax.numpy as jnp
from jax import lax
from jax.sharding import PartitionSpec as P

ROUNDS = 4
NS_STEPS = 3


EPSILON = 1e-06
PRECISE = lax.Precision.HIGHEST


def shifted(block, axis, distance):
    devices = range(lax.axis_size(axis))
    route = [(i - distance, i) for i in devices if i - distance in devices]
    return lax.ppermute(block, axis, route)


def make_rotation(cross_block, column_norms):
    block_width = cross_block.shape[0]
    upper_norm = column_norms[:block_width][:, None]
    lower_norm = column_norms[block_width:][None, :]
    spread = lower_norm - upper_norm
    coupling = (
        cross_block
        * spread
        / (spread * spread + 4.0 * cross_block * cross_block + upper_norm * lower_norm + EPSILON)
    )
    blank_block = jnp.zeros((block_width, block_width), jnp.float32)
    generator = jnp.concatenate(
        [
            jnp.concatenate([blank_block, coupling], 1),
            jnp.concatenate([-coupling.T, blank_block], 1),
        ],
        0,
    )
    damping = 1.0 / jnp.sqrt(1.0 + 2.0 * jnp.sum(coupling * coupling))
    rotation = (jnp.eye(2 * block_width, dtype=jnp.float32) + generator) * damping
    for iteration in range(NS_STEPS):
        product = lax.dot_general(
            rotation,
            rotation,
            (((0,), (0,)), ((), ())),
            precision=PRECISE,
            preferred_element_type=jnp.float32,
        )
        rotation = 1.5 * rotation - 0.5 * jnp.dot(
            rotation, product, precision=PRECISE, preferred_element_type=jnp.float32
        )
    return rotation


def inner_rows(left_rows, right_rows):
    return lax.dot_general(
        left_rows,
        right_rows,
        (((1,), (1,)), ((), ())),
        precision=PRECISE,
        preferred_element_type=jnp.float32,
    )


def body(snapshots, live_rows):
    rows_local = snapshots.shape[1]
    block_width = snapshots.shape[0] // 2
    slot_index = lax.broadcasted_iota(jnp.int32, (1, rows_local), 1)
    current = jnp.where(slot_index < live_rows[0], snapshots, jnp.zeros((), jnp.float32))
    pair_index = lax.axis_index("pair")
    last_index = lax.axis_size("pair") - 1
    for round_index in range(ROUNDS):
        cross_block = inner_rows(current[:block_width], current[block_width:])
        column_norms = jnp.sum(current * current, axis=1)
        cross_block, column_norms = lax.psum((cross_block, column_norms), "row")
        rotation = make_rotation(cross_block, column_norms)
        current = lax.dot_general(
            rotation,
            current,
            (((0,), (0,)), ((), ())),
            precision=PRECISE,
            preferred_element_type=jnp.float32,
        )
        if round_index + 1 < ROUNDS:
            upper_block = current[:block_width]
            lower_block = current[block_width:]
            outgoing = jnp.where(pair_index == 0, lower_block, upper_block)
            arrived_top = shifted(outgoing, "pair", 1)
            arrived_bottom = shifted(lower_block, "pair", -1)
            new_top = jnp.where(pair_index == 0, upper_block, arrived_top)
            new_bottom = jnp.where(pair_index == last_index, upper_block, arrived_bottom)
            current = jnp.concatenate([new_top, new_bottom], 0)
    return current


def solution(mesh):
    return jax.shard_map(
        body,
        mesh=mesh,
        in_specs=(P("pair", "row"), P("row")),
        out_specs=P("pair", "row"),
        check_vma=False,
    )
```

profile of v0, /device:TPU:0, one launch (start us, length us, event | category | flops | bytes accessed | tf_op | source)
XLA Modules:
  0.0 230.5 jit_solution(2087802421568311742)
XLA Ops:
  0.7 2.0 multiply_reduce_fusion.3
  2.6 1.0 fusion.15
  3.6 13.2 %all-reduce.11 = (f32[64,64]{1,0:T(8,128)S(1)}, f32[128]{0:T(128)S(1)}) all-reduce(f32[64,64]{1,0:T(8,128)S(1)} %fusion.15, f32[128]{0:T(128)S(1)} %get-tuple-element.21), channel_id=1, replica_groups=mesh['pair'=8,'row'=4] {'row'}, use_global_device_ids=true, to_apply=%region_0.1 | all-reduce | flops 4224 | bytes 33792 | tf_op jit(solution)/shard_map/psum | solution.py:74
  16.9 0.7 multiply_reduce_fusion.7
  20.1 3.2 %fusion.90 = f32[128,4096]{1,0:T(8,128)} fusion(f32[128,128]{0,1:T(8,128)S(1)} %fusion.12, f32[128,4096]{1,0:T(8,128)S(1)} %get-tuple-element.22), kind=kOutput, calls=%fused_computation.139 | convolution fusion | flops 805306368 | bytes 4259840 | tf_op jit(solution)/shard_map/dot_general | solution.py:76
  23.3 1.7 fusion.83
  25.0 1.3 collective-permute-start.1
  26.3 5.5 %collective-permute-start = (f32[64,4096]{1,0:T(8,128)S(1)}, f32[64,4096]{1,0:T(8,128)}, u32[]{:S(2)}, u32[]{:S(2)}) collective-permute-start(f32[64,4096]{1,0:T(8,128)S(1)} %get-tuple-element.34), channel_id=1, source_target_pairs={{0,4},{4,8},{8,12},{12,16},{16,20},{20,24},{24,28},{1,5},{5,9},{9,... | collective-permute-start | bytes 3145736 | tf_op jit(solution)/shard_map/ppermute | solution.py:17
  31.9 18.8 %collective-permute-done.1 = f32[64,4096]{1,0:T(8,128)S(1)} collective-permute-done((f32[64,4096]{1,0:T(8,128)S(1)}, f32[64,4096]{1,0:T(8,128)S(1)}, u32[]{:S(2)}, u32[]{:S(2)}) %collective-permute-start.1) | collective-permute-done | bytes 1048608 | tf_op jit(solution)/shard_map/ppermute | solution.py:17
  50.7 22.6 %collective-permute-done = f32[64,4096]{1,0:T(8,128)} collective-permute-done((f32[64,4096]{1,0:T(8,128)S(1)}, f32[64,4096]{1,0:T(8,128)}, u32[]{:S(2)}, u32[]{:S(2)}) %collective-permute-start) | collective-permute-done | bytes 1048608 | tf_op jit(solution)/shard_map/ppermute | solution.py:17
  73.2 1.4 slice_select_fusion.6
  74.9 1.0 fusion.91
  75.9 11.9 %all-reduce.10 = (f32[64,64]{1,0:T(8,128)S(1)}, f32[128]{0:T(128)S(1)}) all-reduce(f32[64,64]{1,0:T(8,128)S(1)} %fusion.91, f32[128]{0:T(128)S(1)} %multiply_reduce_fusion.2), channel_id=1, replica_groups=mesh['pair'=8,'row'=4] {'row'}, use_global_device_ids=true, to_apply=%region_4.5 | all-reduce | flops 4224 | bytes 33792 | tf_op jit(solution)/shard_map/psum | solution.py:74
  87.8 0.7 multiply_reduce_fusion.6
  91.1 1.9 fusion.2
  93.2 1.3 collective-permute-start.3
  94.5 5.5 %collective-permute-start.2 = (f32[64,4096]{1,0:T(8,128)S(1)}, f32[64,4096]{1,0:T(8,128)S(1)}, u32[]{:S(2)}, u32[]{:S(2)}) collective-permute-start(f32[64,4096]{1,0:T(8,128)S(1)} %get-tuple-element.30), channel_id=1, source_target_pairs={{0,4},{4,8},{8,12},{12,16},{16,20},{20,24},{24,28},{1,5},{5,9},{9,... | collective-permute-start | bytes 3145736 | tf_op jit(solution)/shard_map/ppermute | solution.py:17
  100.0 20.1 %collective-permute-done.3 = f32[64,4096]{1,0:T(8,128)S(1)} collective-permute-done((f32[64,4096]{1,0:T(8,128)S(1)}, f32[64,4096]{1,0:T(8,128)S(1)}, u32[]{:S(2)}, u32[]{:S(2)}) %collective-permute-start.3) | collective-permute-done | bytes 1048608 | tf_op jit(solution)/shard_map/ppermute | solution.py:17
  120.1 22.6 %collective-permute-done.2 = f32[64,4096]{1,0:T(8,128)S(1)} collective-permute-done((f32[64,4096]{1,0:T(8,128)S(1)}, f32[64,4096]{1,0:T(8,128)S(1)}, u32[]{:S(2)}, u32[]{:S(2)}) %collective-permute-start.2) | collective-permute-done | bytes 1048608 | tf_op jit(solution)/shard_map/ppermute | solution.py:17
  143.1 1.0 fusion.94
  144.1 11.9 %all-reduce.9 = (f32[64,64]{1,0:T(8,128)S(1)}, f32[128]{0:T(128)S(1)}) all-reduce(f32[64,64]{1,0:T(8,128)S(1)} %fusion.94, f32[128]{0:T(128)S(1)} %multiply_reduce_fusion.1), channel_id=1, replica_groups=mesh['pair'=8,'row'=4] {'row'}, use_global_device_ids=true, to_apply=%region_8.9 | all-reduce | flops 4224 | bytes 33792 | tf_op jit(solution)/shard_map/psum | solution.py:74
  156.1 0.7 multiply_reduce_fusion.5
  157.5 0.3 fusion.41
  159.3 1.9 fusion.1
  161.4 1.3 collective-permute-start.5
  162.7 5.1 %collective-permute-start.4 = (f32[64,4096]{1,0:T(8,128)S(1)}, f32[64,4096]{1,0:T(8,128)S(1)}, u32[]{:S(2)}, u32[]{:S(2)}) collective-permute-start(f32[64,4096]{1,0:T(8,128)S(1)} %get-tuple-element.26), channel_id=1, source_target_pairs={{0,4},{4,8},{8,12},{12,16},{16,20},{20,24},{24,28},{1,5},{5,9},{9,... | collective-permute-start | bytes 3145736 | tf_op jit(solution)/shard_map/ppermute | solution.py:17
  167.8 20.2 %collective-permute-done.5 = f32[64,4096]{1,0:T(8,128)S(1)} collective-permute-done((f32[64,4096]{1,0:T(8,128)S(1)}, f32[64,4096]{1,0:T(8,128)S(1)}, u32[]{:S(2)}, u32[]{:S(2)}) %collective-permute-start.5) | collective-permute-done | bytes 1048608 | tf_op jit(solution)/shard_map/ppermute | solution.py:17
  188.0 22.6 %collective-permute-done.4 = f32[64,4096]{1,0:T(8,128)S(1)} collective-permute-done((f32[64,4096]{1,0:T(8,128)S(1)}, f32[64,4096]{1,0:T(8,128)S(1)}, u32[]{:S(2)}, u32[]{:S(2)}) %collective-permute-start.4) | collective-permute-done | bytes 1048608 | tf_op jit(solution)/shard_map/ppermute | solution.py:17
  211.0 1.0 fusion.97
  212.0 11.9 %all-reduce.8 = (f32[64,64]{1,0:T(8,128)S(1)}, f32[128]{0:T(128)S(1)}) all-reduce(f32[64,64]{1,0:T(8,128)S(1)} %fusion.97, f32[128]{0:T(128)S(1)} %multiply_reduce_fusion), channel_id=1, replica_groups=mesh['pair'=8,'row'=4] {'row'}, use_global_device_ids=true, to_apply=%region_12.13 | all-reduce | flops 4224 | bytes 33792 | tf_op jit(solution)/shard_map/psum | solution.py:74
  224.0 0.7 multiply_reduce_fusion.4
  227.3 3.2 %fusion = f32[128,4096]{1,0:T(8,128)} fusion(f32[128,128]{0,1:T(8,128)S(1)} %fusion.3, f32[64,4096]{1,0:T(8,128)S(1)} %get-tuple-element.23, f32[64,4096]{1,0:T(8,128)S(1)} %get-tuple-element.24), kind=kOutput, calls=%fused_computation.7 | convolution fusion | flops 805830656 | bytes 4259840 | tf_op jit(solution)/shard_map/dot_general | solution.py:76
  (43 shorter events, 8.7 us)
Async XLA Ops:
  25.0 25.6 %collective-permute-start.1 = (f32[64,4096]{1,0:T(8,128)S(1)}, f32[64,4096]{1,0:T(8,128)S(1)}, u32[]{:S(2)}, u32[]{:S(2)}) collective-permute-start(f32[64,4096]{1,0:T(8,128)S(1)} %get-tuple-element.33), channel_id=1, source_target_pairs={{4,0},{8,4},{12,8},{16,12},{20,16},{24,20},{28,24},{5,1},{9,5},{13... | collective-permute-start | bytes 3145736 | tf_op jit(solution)/shard_map/ppermute | solution.py:17
  26.3 46.9 %collective-permute-start = (f32[64,4096]{1,0:T(8,128)S(1)}, f32[64,4096]{1,0:T(8,128)}, u32[]{:S(2)}, u32[]{:S(2)}) collective-permute-start(f32[64,4096]{1,0:T(8,128)S(1)} %get-tuple-element.34), channel_id=1, source_target_pairs={{0,4},{4,8},{8,12},{12,16},{16,20},{20,24},{24,28},{1,5},{5,9},{9,... | collective-permute-start | bytes 3145736 | tf_op jit(solution)/shard_map/ppermute | solution.py:17
  93.2 26.9 %collective-permute-start.3 = (f32[64,4096]{1,0:T(8,128)S(1)}, f32[64,4096]{1,0:T(8,128)S(1)}, u32[]{:S(2)}, u32[]{:S(2)}) collective-permute-start(f32[64,4096]{1,0:T(8,128)S(1)} %get-tuple-element.29), channel_id=1, source_target_pairs={{4,0},{8,4},{12,8},{16,12},{20,16},{24,20},{28,24},{5,1},{9,5},{13... | collective-permute-start | bytes 3145736 | tf_op jit(solution)/shard_map/ppermute | solution.py:17
  94.5 48.2 %collective-permute-start.2 = (f32[64,4096]{1,0:T(8,128)S(1)}, f32[64,4096]{1,0:T(8,128)S(1)}, u32[]{:S(2)}, u32[]{:S(2)}) collective-permute-start(f32[64,4096]{1,0:T(8,128)S(1)} %get-tuple-element.30), channel_id=1, source_target_pairs={{0,4},{4,8},{8,12},{12,16},{16,20},{20,24},{24,28},{1,5},{5,9},{9,... | collective-permute-start | bytes 3145736 | tf_op jit(solution)/shard_map/ppermute | solution.py:17
  161.4 26.6 %collective-permute-start.5 = (f32[64,4096]{1,0:T(8,128)S(1)}, f32[64,4096]{1,0:T(8,128)S(1)}, u32[]{:S(2)}, u32[]{:S(2)}) collective-permute-start(f32[64,4096]{1,0:T(8,128)S(1)} %get-tuple-element.25), channel_id=1, source_target_pairs={{4,0},{8,4},{12,8},{16,12},{20,16},{24,20},{28,24},{5,1},{9,5},{13... | collective-permute-start | bytes 3145736 | tf_op jit(solution)/shard_map/ppermute | solution.py:17
  162.7 47.9 %collective-permute-start.4 = (f32[64,4096]{1,0:T(8,128)S(1)}, f32[64,4096]{1,0:T(8,128)S(1)}, u32[]{:S(2)}, u32[]{:S(2)}) collective-permute-start(f32[64,4096]{1,0:T(8,128)S(1)} %get-tuple-element.26), channel_id=1, source_target_pairs={{0,4},{4,8},{8,12},{12,16},{16,20},{20,24},{24,28},{1,5},{5,9},{9,... | collective-permute-start | bytes 3145736 | tf_op jit(solution)/shard_map/ppermute | solution.py:17
where the time goes:
time: 231 us
  waiting for transfers between devices  127 us (55%)
  blocking collectives  48.8 us (21%)
  matrix products  21.3 us (9%)
  starting transfers between devices  20 us (9%)
  other arithmetic  9.18 us (4%)
  between operations  3.75 us (2%)
    ppermute x6, waiting for transfers between devices, shifted(): return lax.ppermute(block, axis, route)  127 us
    psum x4, blocking collectives, body(): cross_block, column_norms = lax.psum((cross_block, column_norms), 'row')  48.8 us
    ppermute x6, starting transfers between devices, shifted(): return lax.ppermute(block, axis, route)  20 us
    dot_general x4, matrix products, body(): lax.dot_general(rotation, current, (((0,), (0,)), ((), ())), precision=PR...  10.2 us
  transfers between devices with their start and end apart: 6, of which 6 were waited for; matrix products, arithmetic and copies ran while one was open for 0% of the time, Pallas kernels for 0%

commit v1 on v0

v1 whole, which is shorter than its diff:
```python
import functools

import jax
import jax.numpy as jnp
from jax import lax
from jax.experimental import pallas as pl
from jax.experimental.pallas import tpu as pltpu
from jax.sharding import PartitionSpec as P

ROUNDS = 4
NS_STEPS = 3
EPSILON = 1e-06
PRECISE = lax.Precision.HIGHEST
MESH = pl.DeviceIdType.MESH
CHUNKS = 4


def nt(left, right):
    return lax.dot_general(
        left,
        right,
        (((1,), (1,)), ((), ())),
        precision=PRECISE,
        preferred_element_type=jnp.float32,
    )


def nn(left, right):
    return jnp.dot(left, right, precision=PRECISE, preferred_element_type=jnp.float32)


def eye_mask(rows, columns):
    row = lax.broadcasted_iota(jnp.int32, (rows, columns), 0)
    column = lax.broadcasted_iota(jnp.int32, (rows, columns), 1)
    return row == column


def pack(grams, width):
    full = 2 * width
    lane = lax.broadcasted_iota(jnp.int32, (width, full), 1)
    line = lax.broadcasted_iota(jnp.int32, (8, full), 0)
    diagonal = eye_mask(full, full)
    norms = [jnp.sum(jnp.where(diagonal, g, 0.0), axis=0, keepdims=True) for g in grams]
    cross = grams[0][:width]
    tail = jnp.where(line == 0, norms[0], 0.0)
    if len(grams) == 2:
        cross = jnp.where(lane < width, pltpu.roll(grams[1][:width], width, 1), cross)
        tail = jnp.where(line == 1, norms[1], tail)
    return cross, tail


def rotation_transposed(cross, norms, width):
    full = 2 * width
    lane = lax.broadcasted_iota(jnp.int32, (width, full), 1)
    cross = jnp.where(lane >= width, cross, 0.0)
    upper = jnp.sum(jnp.where(eye_mask(width, full), norms, 0.0), axis=1, keepdims=True)
    spread = norms - upper
    coupling = cross * spread / (spread * spread + 4.0 * cross * cross + upper * norms + EPSILON)
    squares = jnp.sum(jnp.sum(coupling * coupling, axis=1, keepdims=True), axis=0, keepdims=True)
    damping = 1.0 / jnp.sqrt(1.0 + 2.0 * squares)
    corner = jnp.concatenate([coupling, jnp.zeros((width, full), jnp.float32)], 0)
    identity = jnp.where(eye_mask(full, full), 1.0, 0.0)
    return (identity - corner + corner.T) * damping


def orthogonalised(turns):
    for _ in range(NS_STEPS):
        products = [nt(t, t) for t in turns]
        turns = [1.5 * t - 0.5 * nn(g, t) for t, g in zip(turns, products)]
    return turns


def kernel(
    pairs, rows, live_ref, x_ref, out_ref, sent0, held1, sent1, held2, sent2, held3, grams,
    gram_send, gram_recv, send1, recv1, send2, recv2, send3, recv3,
):
    p, r = lax.axis_index("pair"), lax.axis_index("row")
    plane, y = p // 2, p % 2
    last_plane = pairs // 2 - 1
    width = x_ref.shape[0] // 2
    cells = x_ref.shape[1]
    half = cells // 2
    step = half // CHUNKS
    first, last = plane == 0, plane == last_plane

    barrier = pltpu.get_barrier_semaphore()
    for k in range(1, 2 * rows):
        other = lax.rem(y * rows + r + k, 2 * rows)
        pl.semaphore_signal(
            barrier, inc=1, device_id=(2 * plane + other // rows, lax.rem(other, rows)), device_id_type=MESH
        )
    for side in range(2):
        @pl.when(plane > 0)
        def _():
            pl.semaphore_signal(barrier, inc=1, device_id=(2 * plane - 2 + side, r), device_id_type=MESH)

        @pl.when(plane < last_plane)
        def _():
            pl.semaphore_signal(barrier, inc=1, device_id=(2 * plane + 2 + side, r), device_id_type=MESH)
    near = jnp.where(plane > 0, 2, 0) + jnp.where(plane < last_plane, 2, 0)
    pl.semaphore_wait(barrier, 2 * rows - 1 + near)

    def columns(h, c):
        return pl.ds(h * half + c * step, step)

    def summed(round_index, gram_list):
        cross, tail = pack(gram_list, width)
        plane_wide = len(gram_list) == 2
        count = 2 * rows if plane_wide else rows
        me = y * rows + r if plane_wide else r
        grams[round_index, me, pl.ds(0, width)] = cross
        grams[round_index, me, pl.ds(width, 8)] = tail
        copies = []
        for k in range(1, count):
            other = lax.rem(me + k, count)
            target = (2 * plane + other // rows, lax.rem(other, rows)) if plane_wide else (p, other)
            copy = pltpu.make_async_remote_copy(
                src_ref=grams.at[round_index, me],
                dst_ref=grams.at[round_index, me],
                send_sem=gram_send.at[round_index, k],
                recv_sem=gram_recv.at[round_index, k],
                device_id=target,
                device_id_type=MESH,
            )
            copy.start()
            copies.append(copy)
        for copy in copies:
            copy.wait()
        total = grams[round_index, 0]
        for k in range(1, count):
            total = total + grams[round_index, k]
        turns = [rotation_transposed(total[:width], total[width : width + 1], width)]
        if plane_wide:
            turns.append(
                rotation_transposed(pltpu.roll(total[:width], width, 1), total[width + 1 : width + 2], width)
            )
        return orthogonalised(turns)

    def goes_to(pair, side):
        if side == 0:
            pair_to = jnp.where(pair == 0, 0, jnp.where(pair == pairs - 1, pairs - 1, pair + 1))
            side_to = jnp.where(pair == pairs - 1, 1, 0)
        else:
            pair_to = jnp.where(pair == 0, 1, pair - 1)
            side_to = jnp.where(pair == 0, 0, 1)
        return pair_to, side_to

    came_from = [
        jnp.where(first, 0, 2 * plane - 1),
        2 * plane + 1,
        2 * plane,
        jnp.where(last, 2 * plane + 1, 2 * plane + 2),
    ]

    def start(local, source, target, send_sem, recv_sem, pair_to):
        @pl.when(local)
        def _():
            pltpu.make_async_copy(source, target, recv_sem).start()

        @pl.when(jnp.logical_not(local))
        def _():
            remote(source, target, send_sem, recv_sem, pair_to).start()

    def remote(source, target, send_sem, recv_sem, pair_to):
        return pltpu.make_async_remote_copy(
            src_ref=source,
            dst_ref=target,
            send_sem=send_sem,
            recv_sem=recv_sem,
            device_id=(pair_to, r),
            device_id_type=MESH,
        )

    def wait_arrival(source, target, recv_sem):
        pltpu.make_async_copy(source, target, recv_sem).wait()

    def wait_sent(local, source, target, send_sem, recv_sem, pair_to):
        @pl.when(jnp.logical_not(local))
        def _():
            remote(source, target, send_sem, recv_sem, pair_to).wait_send()

    live = live_ref[0]

    def masked(h, c):
        slot = lax.broadcasted_iota(jnp.int32, (1, step), 1) + (h * half + c * step)
        return jnp.where(slot < live, x_ref[:, columns(h, c)], 0.0)

    gram = jnp.zeros((2 * width, 2 * width), jnp.float32)
    for h in range(2):
        for c in range(CHUNKS):
            block = masked(h, c)
            gram = gram + nt(block, block)
    (turn,) = summed(0, [gram])

    def move1(side, h, c):
        pair_to, side_to = goes_to(p, side)
        slot = 2 * lax.rem(pair_to, 2) + side_to
        device = 2 * (pair_to // 2) + h
        part = pl.ds(c * step, step)
        return (
            device == p,
            sent0.at[h, side, :, part],
            held1.at[slot, :, part],
            send1.at[side, h, c],
            recv1.at[slot, c],
            device,
        )

    for c in range(CHUNKS):
        for h in range(2):
            result = nn(turn, masked(h, c))
            sent0[h, :, :, pl.ds(c * step, step)] = result.reshape(2, width, step)
            for side in range(2):
                start(*move1(side, h, c))

    def plane_round(round_index, held, recv):
        gram_list = [jnp.zeros((2 * width, 2 * width), jnp.float32)] * 2
        for c in range(CHUNKS):
            part = pl.ds(c * step, step)
            for slot in range(4):
                wait_arrival(held.at[slot, :, part], held.at[slot, :, part], recv.at[slot, c])
            for which in range(2):
                block = held[2 * which : 2 * which + 2, :, part].reshape(2 * width, step)
                gram_list[which] = gram_list[which] + nt(block, block)
        return summed(round_index, gram_list)

    def rotated(turns, held, sent, c):
        part = pl.ds(c * step, step)
        for which in range(2):
            block = held[2 * which : 2 * which + 2, :, part].reshape(2 * width, step)
            sent[2 * which : 2 * which + 2, :, part] = nn(turns[which], block).reshape(2, width, step)

    def move2(pair_side, c):
        which, side = pair_side // 2, pair_side % 2
        pair_to, side_to = goes_to(2 * plane + which, side)
        slot = 2 * lax.rem(pair_to, 2) + side_to
        device = 2 * (pair_to // 2) + y
        part = pl.ds(c * step, step)
        return (
            device == p,
            sent1.at[pair_side, :, part],
            held2.at[slot, :, part],
            send2.at[pair_side, c],
            recv2.at[slot, c],
            device,
        )

    def move3(pair_side, c):
        which, side = pair_side // 2, pair_side % 2
        pair_to, side_to = goes_to(2 * plane + which, side)
        part = pl.ds(c * step, step)
        return (
            pair_to == p,
            sent2.at[pair_side, :, part],
            held3.at[y, side_to, :, part],
            send3.at[pair_side, c],
            recv3.at[y, side_to, c],
            pair_to,
        )

    turns = plane_round(1, held1, recv1)
    for c in range(CHUNKS):
        rotated(turns, held1, sent1, c)
        for pair_side in range(4):
            start(*move2(pair_side, c))
    turns = plane_round(2, held2, recv2)
    for c in range(CHUNKS):
        rotated(turns, held2, sent2, c)
        for pair_side in range(4):
            start(*move3(pair_side, c))

    gram = jnp.zeros((2 * width, 2 * width), jnp.float32)
    for c in range(CHUNKS):
        part = pl.ds(c * step, step)
        for h in range(2):
            for side in range(2):
                ref = held3.at[h, side, :, part]
                wait_arrival(ref, ref, recv3.at[h, side, c])
            block = held3[h, :, :, part].reshape(2 * width, step)
            gram = gram + nt(block, block)
    (turn,) = summed(3, [gram])
    for h in range(2):
        for c in range(CHUNKS):
            block = held3[h, :, :, pl.ds(c * step, step)].reshape(2 * width, step)
            out_ref[:, columns(h, c)] = nn(turn, block)

    for c in range(CHUNKS):
        for side in range(2):
            for h in range(2):
                wait_sent(*move1(side, h, c))
        for pair_side in range(4):
            wait_sent(*move2(pair_side, c))
            wait_sent(*move3(pair_side, c))


def solution(mesh):
    pairs, rows = mesh.shape["pair"], mesh.shape["row"]

    def body(snapshots, live_rows):
        full, cells = snapshots.shape
        width, half = full // 2, cells // 2
        state = pltpu.VMEM((4, width, half), jnp.float32)
        stated = pltpu.VMEM((2, 2, width, half), jnp.float32)
        return pl.pallas_call(
            functools.partial(kernel, pairs, rows),
            out_shape=jax.ShapeDtypeStruct(snapshots.shape, jnp.float32),
            in_specs=[
                pl.BlockSpec(memory_space=pltpu.SMEM),
                pl.BlockSpec(memory_space=pltpu.VMEM),
            ],
            out_specs=pl.BlockSpec(memory_space=pltpu.VMEM),
            scratch_shapes=[
                stated,
                state,
                state,
                state,
                state,
                stated,
                pltpu.VMEM((ROUNDS, 2 * rows, width + 8, full), jnp.float32),
                pltpu.SemaphoreType.DMA((ROUNDS, 2 * rows)),
                pltpu.SemaphoreType.DMA((ROUNDS, 2 * rows)),
                pltpu.SemaphoreType.DMA((2, 2, CHUNKS)),
                pltpu.SemaphoreType.DMA((4, CHUNKS)),
                pltpu.SemaphoreType.DMA((4, CHUNKS)),
                pltpu.SemaphoreType.DMA((4, CHUNKS)),
                pltpu.SemaphoreType.DMA((4, CHUNKS)),
                pltpu.SemaphoreType.DMA((2, 2, CHUNKS)),
            ],
            compiler_params=pltpu.CompilerParams(
                collective_id=0, has_side_effects=True, vmem_limit_bytes=48 * 1024 * 1024
            ),
        )(live_rows, snapshots)

    return jax.shard_map(
        body,
        mesh=mesh,
        in_specs=(P("pair", "row"), P("row")),
        out_specs=P("pair", "row"),
        check_vma=False,
    )
```

time: 231 us -> 125 us (0.54)
  the two profiles are of different devices: /device:TPU:0 before, /device:TPU:17 now
where the time goes in v1:
time: 125 us
  Pallas kernels  121 us (97%)
  local copies, waits for them, and re-layouts  2.91 us (2%)
    pallas_call x1, Pallas kernels, body(): pl.pallas_call(functools.partial(kernel, pairs, rows), out_shape=jax.Shap...  121 us
    unnamed x3, local copies, waits for them, and re-layouts  2.91 us

profile of v1, /device:TPU:17, one launch (start us, length us, event | category | flops | bytes accessed | tf_op | source)
XLA Modules:
  0.0 125.0 jit_solution(18266716162897620576)
XLA Ops:
  0.7 0.0 copy-start
  0.7 1.6 %copy-done = f32[128,4096]{1,0:T(8,128)S(1)} copy-done((f32[128,4096]{1,0:T(8,128)S(1)}, f32[128,4096]{1,0:T(8,128)}, u32[]{:S(2)}) %copy-start) | copy-done | bytes 2097176
  2.2 121.4 %shard_map.28 = f32[128,4096]{1,0:T(8,128)S(1)} custom-call(s32[1]{0:T(128)S(6)} %copy.4.live_ref, f32[128,4096]{1,0:T(8,128)S(1)} %copy-done), custom_call_target="tpu_custom_call" | custom-call | tf_op jit(solution)/shard_map/pallas_call | solution.py:304
  123.7 1.3 %copy.5 = f32[128,4096]{1,0:T(8,128)} copy(f32[128,4096]{1,0:T(8,128)S(1)} %shard_map.28) | data formatting | bytes 4194304
Async XLA Ops:
  0.7 1.6 %copy-start = (f32[128,4096]{1,0:T(8,128)S(1)}, f32[128,4096]{1,0:T(8,128)}, u32[]{:S(2)}) copy-start(f32[128,4096]{1,0:T(8,128)} %x_ref.1) | copy-start | bytes 6291460

commit v2 on v0

v2 whole, which is shorter than its diff:
```python
import functools

import jax
import jax.numpy as jnp
from jax import lax
from jax.experimental import pallas as pl
from jax.experimental.pallas import tpu as pltpu
from jax.sharding import PartitionSpec as P

ROUNDS = 4
NS_STEPS = 3
EPSILON = 1e-06
PRECISE = lax.Precision.HIGHEST
MESH = pl.DeviceIdType.MESH
CHUNKS = 4
EARLY = 1
LATE = 1


def nt(left, right):
    return lax.dot_general(
        left,
        right,
        (((1,), (1,)), ((), ())),
        precision=PRECISE,
        preferred_element_type=jnp.float32,
    )


def nn(left, right):
    return jnp.dot(left, right, precision=PRECISE, preferred_element_type=jnp.float32)


def eye_mask(rows, columns):
    row = lax.broadcasted_iota(jnp.int32, (rows, columns), 0)
    column = lax.broadcasted_iota(jnp.int32, (rows, columns), 1)
    return row == column


def halves(block):
    high = block.astype(jnp.bfloat16)
    return high, (block - high.astype(jnp.float32)).astype(jnp.bfloat16)


def gram_parts(block):
    high, low = halves(block)
    return lax.dot_general(
        high,
        jnp.concatenate([high, low], 0),
        (((1,), (1,)), ((), ())),
        preferred_element_type=jnp.float32,
    )


def gram_of(parts):
    full = parts.shape[0]
    mixed = parts[:, full:]
    return parts[:, :full] + mixed + mixed.T


def turn_halves(turn):
    high, low = halves(turn)
    return jnp.concatenate([high, high], 1), low


def turned(turn, block):
    wide, low_turn = turn
    high, low = halves(block)
    return jnp.dot(
        wide, jnp.concatenate([high, low], 0), preferred_element_type=jnp.float32
    ) + jnp.dot(low_turn, high, preferred_element_type=jnp.float32)


def norms_of(gram):
    return jnp.sum(jnp.where(eye_mask(*gram.shape), gram, 0.0), axis=0, keepdims=True)


def pack_two(first, second, width):
    lane = lax.broadcasted_iota(jnp.int32, (width, 2 * width), 1)
    line = lax.broadcasted_iota(jnp.int32, (8, 2 * width), 0)
    cross = jnp.where(lane < width, pltpu.roll(second[:width], width, 1), first[:width])
    return cross, jnp.where(line == 0, norms_of(first), norms_of(second))


def pack_one(gram, width):
    part = width // 2
    lane = lax.broadcasted_iota(jnp.int32, (part, 2 * width), 1)
    cross = jnp.where(lane < width, pltpu.roll(gram[:part], width, 1), gram[part:width])
    return cross, jnp.broadcast_to(norms_of(gram), (8, 2 * width))


def rotation_transposed(cross, norms, width):
    full = 2 * width
    lane = lax.broadcasted_iota(jnp.int32, (width, full), 1)
    cross = jnp.where(lane >= width, cross, 0.0)
    upper = jnp.sum(jnp.where(eye_mask(width, full), norms, 0.0), axis=1, keepdims=True)
    spread = norms - upper
    coupling = cross * spread / (spread * spread + 4.0 * cross * cross + upper * norms + EPSILON)
    squares = jnp.sum(jnp.sum(coupling * coupling, axis=1, keepdims=True), axis=0, keepdims=True)
    damping = 1.0 / jnp.sqrt(1.0 + 2.0 * squares)
    corner = jnp.concatenate([coupling, jnp.zeros((width, full), jnp.float32)], 0)
    identity = jnp.where(eye_mask(full, full), 1.0, 0.0)
    return (identity - corner + corner.T) * damping


def orthogonalised(turns):
    for _ in range(NS_STEPS):
        products = [nt(t, t) for t in turns]
        turns = [1.5 * t - 0.5 * nn(g, t) for t, g in zip(turns, products)]
    return turns


def kernel(
    pairs, rows, live_ref, x_hbm, out_ref, x_ref, raw, sent0, held1, sent1, held2, sent2, held3, final,
    turn_out, turn_in, singles, doubles, load_sem, raw_send, raw_recv, turn_sem,
    one_send, one_recv, two_send, two_recv, move_send, move_recv, last_send, last_recv,
):
    p, r = lax.axis_index("pair"), lax.axis_index("row")
    plane, y = p // 2, p % 2
    last_plane = pairs // 2 - 1
    partner = 2 * plane + 1 - y
    full, cells = x_ref.shape
    width = full // 2
    half = cells // 2
    step = half // CHUNKS
    first, last = plane == 0, plane == last_plane

    def columns(h, c):
        return pl.ds(pl.multiple_of(h * half + c * step, step), step)

    def load(k):
        part = pl.ds(k * step, step)
        return pltpu.make_async_copy(x_hbm.at[:, part], x_ref.at[:, part], load_sem.at[k])

    for k in range(2 * CHUNKS):
        load(k).start()

    barrier = pltpu.get_barrier_semaphore()
    for k in range(1, 2 * rows):
        other = lax.rem(y * rows + r + k, 2 * rows)
        pl.semaphore_signal(
            barrier, inc=1, device_id=(2 * plane + other // rows, lax.rem(other, rows)), device_id_type=MESH
        )

    @pl.when(plane > 0)
    def _():
        pl.semaphore_signal(barrier, inc=1, device_id=(p - 2, r), device_id_type=MESH)

    @pl.when(plane < last_plane)
    def _():
        pl.semaphore_signal(barrier, inc=1, device_id=(p + 2, r), device_id_type=MESH)

    near = jnp.where(plane > 0, 1, 0) + jnp.where(plane < last_plane, 1, 0)
    pl.semaphore_wait(barrier, 2 * rows - 1 + near)

    def remote(source, target, send_sem, recv_sem, pair_to, row_to=r):
        return pltpu.make_async_remote_copy(
            src_ref=source,
            dst_ref=target,
            send_sem=send_sem,
            recv_sem=recv_sem,
            device_id=(pair_to, row_to),
            device_id_type=MESH,
        )

    def arrived(target, recv_sem):
        pltpu.make_async_copy(target, target, recv_sem).wait()

    def raw_copy(c):
        return remote(
            x_hbm.at[:, columns(1 - y, c)], raw.at[:, pl.ds(c * step, step)], raw_send.at[c], raw_recv.at[c], partner
        )

    def share(buffer, slot, me, count, send_sem, recv_sem, target):
        copies = []
        for k in range(1, count):
            other = lax.rem(me + k, count)
            copy = remote(
                buffer.at[slot, me], buffer.at[slot, me], send_sem.at[slot, k], recv_sem.at[slot, k], *target(other)
            )
            copy.start()
            copies.append(copy)
        return copies

    def total(buffer, slot, count, copies):
        for copy in copies:
            copy.wait()
        result = buffer[slot, 0]
        for k in range(1, count):
            result = result + buffer[slot, k]
        return result

    def share_one(slot, gram):
        cross, tail = pack_one(gram, width)
        singles[slot, r, pl.ds(0, width // 2)] = cross
        singles[slot, r, pl.ds(width // 2, 8)] = tail
        return share(singles, slot, r, rows, one_send, one_recv, lambda other: (p, other))

    def turn_one(slot, copies):
        part = width // 2
        result = total(singles, slot, rows, copies)
        cross = jnp.concatenate([pltpu.roll(result[:part], width, 1), result[:part]], 0)
        return orthogonalised([rotation_transposed(cross, result[part : part + 1], width)])[0]

    def turn_two(slot, grams):
        cross, tail = pack_two(grams[0], grams[1], width)
        me = y * rows + r
        doubles[slot, me, pl.ds(0, width)] = cross
        doubles[slot, me, pl.ds(width, 8)] = tail
        copies = share(
            doubles, slot, me, 2 * rows, two_send, two_recv,
            lambda other: (2 * plane + other // rows, lax.rem(other, rows)),
        )
        result = total(doubles, slot, 2 * rows, copies)
        return orthogonalised([
            rotation_transposed(result[:width], result[width : width + 1], width),
            rotation_transposed(pltpu.roll(result[:width], width, 1), result[width + 1 : width + 2], width),
        ])

    def goes_to(pair, side):
        if side == 0:
            pair_to = jnp.where(pair == 0, 0, jnp.where(pair == pairs - 1, pairs - 1, pair + 1))
            side_to = jnp.where(pair == pairs - 1, 1, 0)
        else:
            pair_to = jnp.where(pair == 0, 1, pair - 1)
            side_to = jnp.where(pair == 0, 0, 1)
        return pair_to, side_to

    def move(number, sent, held, which, side, c):
        pair_to, side_to = goes_to(2 * plane + which, side)
        slot = 2 * lax.rem(pair_to, 2) + side_to
        device = 2 * (pair_to // 2) + y
        part = pl.ds(c * step, step)
        source = sent.at[2 * which + side, :, part]
        target = held.at[slot, :, part]
        recv_sem = move_recv.at[number, slot, c]
        copy = remote(source, target, move_send.at[number, 2 * which + side, c], recv_sem, device)
        return device == p, copy, pltpu.make_async_copy(source, target, recv_sem)

    def start_move(*place):
        local, copy, inside = move(*place)

        @pl.when(local)
        def _():
            inside.start()

        @pl.when(jnp.logical_not(local))
        def _():
            copy.start()

    def end_move(*place):
        local, copy, _ = move(*place)

        @pl.when(jnp.logical_not(local))
        def _():
            copy.wait_send()

    def wait_slots(number, held, slots, c):
        for slot in slots:
            arrived(held.at[slot, :, pl.ds(c * step, step)], move_recv.at[number, slot, c])

    def pair_block(held, which, c):
        return held[pl.ds(2 * which, 2), :, pl.ds(c * step, step)].reshape(full, step)

    live = live_ref[0]

    def masked(block, h, c):
        slot = lax.broadcasted_iota(jnp.int32, (1, step), 1) + (h * half + c * step)
        return jnp.where(slot < live, block, 0.0)

    for c in range(EARLY):
        raw_copy(c).start()
    parts = jnp.zeros((full, 2 * full), jnp.float32)
    for k in range(2 * CHUNKS):
        load(k).wait()
        h, c = k // CHUNKS, k % CHUNKS
        parts = parts + gram_parts(masked(x_ref[:, columns(h, c)], h, c))
    copies = share_one(0, gram_of(parts))
    for c in range(EARLY, CHUNKS - 1):
        raw_copy(c).start()
    turn = turn_one(0, copies)
    turn_out[...] = turn
    turn_copy = remote(turn_out, turn_in, turn_sem.at[0], turn_sem.at[1], partner)
    turn_copy.start()
    for c in range(max(EARLY, CHUNKS - 1), CHUNKS):
        raw_copy(c).start()

    def first_turn(which, turn_parts, block, c):
        sent0[pl.ds(2 * which, 2), :, pl.ds(c * step, step)] = turned(turn_parts, masked(block, y, c)).reshape(
            2, width, step
        )
        for side in range(2):
            for number in range(2):
                @pl.when(which == number)
                def _():
                    start_move(0, sent0, held1, number, side, c)

    own = turn_halves(turn)
    for c in range(CHUNKS):
        first_turn(y, own, x_ref[:, columns(y, c)], c)
    turn_copy.wait()
    other = turn_halves(turn_in[...])
    for c in range(CHUNKS):
        raw_copy(c).wait_recv()
        first_turn(1 - y, other, raw[:, pl.ds(c * step, step)], c)

    def plane_gram(number, held):
        parts = [jnp.zeros((full, 2 * full), jnp.float32)] * 2
        for c in range(CHUNKS):
            wait_slots(number, held, range(4), c)
            parts = [parts[which] + gram_parts(pair_block(held, which, c)) for which in range(2)]
        return [gram_of(part) for part in parts]

    for number, held, sent, held_next in ((0, held1, sent1, held2), (1, held2, sent2, held3)):
        turns = [turn_halves(t) for t in turn_two(number, plane_gram(number, held))]
        for c in range(CHUNKS):
            for which in range(2):
                sent[2 * which : 2 * which + 2, :, pl.ds(c * step, step)] = turned(
                    turns[which], pair_block(held, which, c)
                ).reshape(2, width, step)
                for side in range(2):
                    start_move(number + 1, sent, held_next, which, side, c)

    def hand_back(side, c):
        part = pl.ds(c * step, step)
        return remote(
            held3.at[2 * (1 - y) + side, :, part],
            final.at[side, :, part],
            last_send.at[side, c],
            last_recv.at[side, c],
            partner,
        )

    for c in range(CHUNKS):
        wait_slots(2, held3, (1, 2), c)
        for number in range(2):
            @pl.when(y == number)
            def _():
                hand_back(number, c).start()
    parts = [jnp.zeros((full, 2 * full), jnp.float32)] * 2
    for c in range(CHUNKS):
        wait_slots(2, held3, (0, 3), c)
        if c < LATE:
            for number in range(2):
                @pl.when(y == number)
                def _():
                    hand_back(1 - number, c).start()
        parts = [parts[which] + gram_parts(pair_block(held3, which, c)) for which in range(2)]
    mine, theirs = (jnp.where(y == k, gram_of(parts[0]), gram_of(parts[1])) for k in range(2))
    cross, tail = pack_one(theirs, width)
    singles[2, 0, pl.ds(0, width // 2)] = cross
    singles[2, 0, pl.ds(width // 2, 8)] = tail
    swap = remote(singles.at[2, 0], singles.at[2, 1], turn_sem.at[2], turn_sem.at[3], partner)
    swap.start()
    for c in range(LATE, CHUNKS):
        for number in range(2):
            @pl.when(y == number)
            def _():
                hand_back(1 - number, c).start()
    cross, tail = pack_one(mine, width)
    swap.wait()
    singles[1, r, pl.ds(0, width // 2)] = cross + singles[2, 1, pl.ds(0, width // 2)]
    singles[1, r, pl.ds(width // 2, 8)] = tail + singles[2, 1, pl.ds(width // 2, 8)]
    copies = share(singles, 1, r, rows, one_send, one_recv, lambda other: (p, other))
    own = turn_halves(turn_one(1, copies))
    for c in range(CHUNKS):
        out_ref[:, columns(y, c)] = turned(own, pair_block(held3, y, c))
    for c in range(CHUNKS):
        for side in range(2):
            hand_back(side, c).wait_recv()
        out_ref[:, columns(1 - y, c)] = turned(own, final[:, :, pl.ds(c * step, step)].reshape(full, step))

    for c in range(CHUNKS):
        raw_copy(c).wait_send()
        for which in range(2):
            for side in range(2):
                for number, sent, held in ((0, sent0, held1), (1, sent1, held2), (2, sent2, held3)):
                    end_move(number, sent, held, which, side, c)
        for side in range(2):
            hand_back(side, c).wait_send()


def solution(mesh):
    pairs, rows = mesh.shape["pair"], mesh.shape["row"]

    def body(snapshots, live_rows):
        full, cells = snapshots.shape
        width, half = full // 2, cells // 2
        state = pltpu.VMEM((4, width, half), jnp.float32)
        copies = pltpu.SemaphoreType.DMA
        return pl.pallas_call(
            functools.partial(kernel, pairs, rows),
            out_shape=jax.ShapeDtypeStruct(snapshots.shape, jnp.float32),
            in_specs=[
                pl.BlockSpec(memory_space=pltpu.SMEM),
                pl.BlockSpec(memory_space=pltpu.HBM),
            ],
            out_specs=pl.BlockSpec(memory_space=pltpu.VMEM),
            scratch_shapes=[
                pltpu.VMEM((full, cells), jnp.float32),
                pltpu.VMEM((full, half), jnp.float32),
                state,
                state,
                state,
                state,
                state,
                state,
                pltpu.VMEM((2, width, half), jnp.float32),
                pltpu.VMEM((full, full), jnp.float32),
                pltpu.VMEM((full, full), jnp.float32),
                pltpu.VMEM((3, max(rows, 2), width // 2 + 8, full), jnp.float32),
                pltpu.VMEM((2, 2 * rows, width + 8, full), jnp.float32),
                copies((2 * CHUNKS,)),
                copies((CHUNKS,)),
                copies((CHUNKS,)),
                copies((4,)),
                copies((2, rows)),
                copies((2, rows)),
                copies((2, 2 * rows)),
                copies((2, 2 * rows)),
                copies((3, 4, CHUNKS)),
                copies((3, 4, CHUNKS)),
                copies((2, CHUNKS)),
                copies((2, CHUNKS)),
            ],
            compiler_params=pltpu.CompilerParams(
                collective_id=0, has_side_effects=True, vmem_limit_bytes=48 * 1024 * 1024
            ),
        )(live_rows, snapshots)

    return jax.shard_map(
        body,
        mesh=mesh,
        in_specs=(P("pair", "row"), P("row")),
        out_specs=P("pair", "row"),
        check_vma=False,
    )
```

time: 231 us -> 98.1 us (0.42)
  waiting for transfers between devices: 127 us -> 0 us
  Pallas kernels: 0 us -> 94.4 us
  blocking collectives: 48.8 us -> 0 us
  matrix products: 21.3 us -> 0 us
  starting transfers between devices: 20 us -> 0 us
  other arithmetic: 9.18 us -> 0 us
  between operations: 3.75 us -> 0.67 us
  local copies, waits for them, and re-layouts: 0.58 us -> 2.91 us
    ppermute x6 -> x0, waiting for transfers between devices: 127 us -> none  [shifted(): return lax.ppermute(block, axis, route)]
    pallas_call x0 -> x1, Pallas kernels: none -> 94.4 us  [body(): pl.pallas_call(functools.partial(kernel, pairs, rows), out_shape=jax.Shap...]
    psum x4 -> x0, blocking collectives: 48.8 us -> none  [body(): cross_block, column_norms = lax.psum((cross_block, column_norms), 'row')]
    dot_general x32 -> x0, matrix products: 21.3 us -> none  [the longest x4 10.2 us: body(): lax.dot_general(rotation, current, (((0,), (0,)), ((), ())), precision=PR...]
    ppermute x6 -> x0, starting transfers between devices: 20 us -> none  [shifted(): return lax.ppermute(block, axis, route)]
    reduce_sum x8 -> x0, other arithmetic: 5.42 us -> none  [the longest x4 2.77 us: make_rotation(): damping = 1.0 / jnp.sqrt(1.0 + 2.0 * jnp.sum(coupling * coupling))]
    unnamed x2 -> x3, local copies, waits for them, and re-layouts: 0.15 us -> 2.91 us
  transfers between devices with their start and end apart: 6 -> 0, of which waited for: 6 -> 0; matrix products, arithmetic and copies ran while one was open for 0% -> 0% of each run, Pallas kernels for 0% -> 0%
where the time goes in v2:
time: 98.1 us; the launch traced here: 97.9 us
  Pallas kernels  94.4 us (96%)
  local copies, waits for them, and re-layouts  2.91 us (3%)
    pallas_call x1, Pallas kernels, body(): pl.pallas_call(functools.partial(kernel, pairs, rows), out_shape=jax.Shap...  94.4 us
    unnamed x3, local copies, waits for them, and re-layouts  2.91 us

profile of v2, /device:TPU:0, one launch (start us, length us, event | category | flops | bytes accessed | tf_op | source)
XLA Modules:
  0.0 97.9 jit_solution(11235232451242588782)
XLA Ops:
  0.7 0.0 copy-start
  0.7 1.6 %copy-done = f32[128,4096]{1,0:T(8,128)S(1)} copy-done((f32[128,4096]{1,0:T(8,128)S(1)}, f32[128,4096]{1,0:T(8,128)}, u32[]{:S(2)}) %copy-start) | copy-done | bytes 2097176
  2.2 94.4 %shard_map.28 = f32[128,4096]{1,0:T(8,128)S(1)} custom-call(s32[1]{0:T(128)S(6)} %copy.4.live_ref, f32[128,4096]{1,0:T(8,128)S(1)} %copy-done), custom_call_target="tpu_custom_call" | custom-call | tf_op jit(solution)/shard_map/pallas_call | solution.py:391
  96.6 1.3 %copy.5 = f32[128,4096]{1,0:T(8,128)} copy(f32[128,4096]{1,0:T(8,128)S(1)} %shard_map.28) | data formatting | bytes 4194304
Async XLA Ops:
  0.7 1.6 %copy-start = (f32[128,4096]{1,0:T(8,128)S(1)}, f32[128,4096]{1,0:T(8,128)}, u32[]{:S(2)}) copy-start(f32[128,4096]{1,0:T(8,128)} %x_hbm.1) | copy-start | bytes 6291460

commit v3 on v2

--- a/solution.py
+++ b/solution.py
@@ -10,25 +10,21 @@
 ROUNDS = 4
 NS_STEPS = 3
 EPSILON = 1e-06
-PRECISE = lax.Precision.HIGHEST
 MESH = pl.DeviceIdType.MESH
 CHUNKS = 4
 EARLY = 1
 LATE = 1
 
 
-def nt(left, right):
+def own_product(block):
+    high, low = halves(block)
+    dims = (((1,), (1,)), ((), ()))
     return lax.dot_general(
-        left,
-        right,
-        (((1,), (1,)), ((), ())),
-        precision=PRECISE,
+        jnp.concatenate([high, high], 1),
+        jnp.concatenate([high, low], 1),
+        dims,
         preferred_element_type=jnp.float32,
-    )
-
-
-def nn(left, right):
-    return jnp.dot(left, right, precision=PRECISE, preferred_element_type=jnp.float32)
+    ) + lax.dot_general(low, high, dims, preferred_element_type=jnp.float32)
 
 
 def eye_mask(rows, columns):
@@ -105,8 +101,8 @@
 
 def orthogonalised(turns):
     for _ in range(NS_STEPS):
-        products = [nt(t, t) for t in turns]
-        turns = [1.5 * t - 0.5 * nn(g, t) for t, g in zip(turns, products)]
+        products = [own_product(t) for t in turns]
+        turns = [1.5 * t - 0.5 * turned(turn_halves(g), t) for t, g in zip(turns, products)]
     return turns
 
 
@@ -239,6 +235,9 @@
 
     def start_move(*place):
         local, copy, inside = move(*place)
+        if place[3] == place[4]:
+            inside.start()
+            return
 
         @pl.when(local)
         def _():
@@ -249,6 +248,8 @@
             copy.start()
 
     def end_move(*place):
+        if place[3] == place[4]:
+            return
         local, copy, _ = move(*place)
 
         @pl.when(jnp.logical_not(local))

time: 98.1 us -> 96.1 us (0.980)
  Pallas kernels: 94.4 us -> 92.4 us
    pallas_call x1, Pallas kernels: 94.4 us -> 92.4 us  [body(): pl.pallas_call(functools.partial(kernel, pairs, rows), out_shape=jax.Shap...]
where the time goes in v3:
time: 96.1 us; the launch traced here: 96 us
  Pallas kernels  92.4 us (96%)
  local copies, waits for them, and re-layouts  2.91 us (3%)
    pallas_call x1, Pallas kernels, body(): pl.pallas_call(functools.partial(kernel, pairs, rows), out_shape=jax.Shap...  92.4 us
    unnamed x3, local copies, waits for them, and re-layouts  2.91 us

profile of v3, /device:TPU:0, one launch (start us, length us, event | category | flops | bytes accessed | tf_op | source)
XLA Modules:
  0.0 96.0 jit_solution(6653212538861879505)
XLA Ops:
  0.7 0.0 copy-start
  0.7 1.6 %copy-done = f32[128,4096]{1,0:T(8,128)S(1)} copy-done((f32[128,4096]{1,0:T(8,128)S(1)}, f32[128,4096]{1,0:T(8,128)}, u32[]{:S(2)}) %copy-start) | copy-done | bytes 2097176
  2.2 92.4 %shard_map.28 = f32[128,4096]{1,0:T(8,128)S(1)} custom-call(s32[1]{0:T(128)S(6)} %copy.4.live_ref, f32[128,4096]{1,0:T(8,128)S(1)} %copy-done), custom_call_target="tpu_custom_call" | custom-call | tf_op jit(solution)/shard_map/pallas_call | solution.py:392
  94.6 1.3 %copy.5 = f32[128,4096]{1,0:T(8,128)} copy(f32[128,4096]{1,0:T(8,128)S(1)} %shard_map.28) | data formatting | bytes 4194304
Async XLA Ops:
  0.7 1.6 %copy-start = (f32[128,4096]{1,0:T(8,128)S(1)}, f32[128,4096]{1,0:T(8,128)}, u32[]{:S(2)}) copy-start(f32[128,4096]{1,0:T(8,128)} %x_hbm.1) | copy-start | bytes 6291460
